TPU v7x, 32 devices: a whole 2x2x4 slice. The times are simulated.
32 devices in a mesh: dp: 8 (over z, x), sp: 4 (over y, core).
Axes of the slice: x: 2, y: 2, z: 4, core: 2. Of those that a mesh axis runs over, the one named last changes fastest.
Arguments:
- tokens: bfloat16 [8192, 768], P(('dp', 'sp')), may hold values from -6 to 6
- segment_ids: int32 [8, 1024], P('dp'), may hold values from 0 to 3, never falling along the last dimension, each value on 1 to 512 neighbouring positions
- masked_rows: int32 [2432], P(('dp', 'sp')), may hold values from 0 to 255, as said below
- replacement: bfloat16 [2432, 768], P(('dp', 'sp')), may hold values from -6 to 6
- cotangent: float32 [2432, 768], P(('dp', 'sp')), may hold values from -6 to 6
- w_qkv: bfloat16 [768, 2304], replicated, may hold values from -0.21875 to 0.21875
- w_out_attn: bfloat16 [768, 768], replicated, may hold values from -0.875 to 0.875
- w_in_ff: bfloat16 [768, 6144], replicated, may hold values from -0.21875 to 0.21875
- w_out_ff: bfloat16 [3072, 768], replicated, may hold values from -0.109375 to 0.109375
- gain_one: float32 [768], replicated, may hold values from 0.1 to 1.9
- shift_one: float32 [768], replicated, may hold values from -3 to 3
- gain_two: float32 [768], replicated, may hold values from 0.1 to 1.9
- shift_two: float32 [768], replicated, may hold values from -3 to 3
Outputs:
- layer_out: bfloat16 [8192, 768], P(('dp', 'sp'))
- grad_tokens: float32 [8192, 768], P(('dp', 'sp'))
- grad_replacement: float32 [2432, 768], P(('dp', 'sp'))
- grad_qkv: float32 [768, 2304], P('dp')
- grad_out_attn: float32 [768, 768], P('dp')
- grad_in_ff: float32 [768, 6144], P('dp')
- grad_out_ff: float32 [3072, 768], P('dp')
- grad_gain_one: float32 [768], replicated
- grad_shift_one: float32 [768], replicated
- grad_gain_two: float32 [768], replicated
- grad_shift_two: float32 [768], replicated
Inputs may be any that keep to these rules, and one draw needn't show every extreme that they name: `masked_rows`: within each device's block of 76 entries the rows are distinct and increasing.
All inputs are finite; a program needn't handle non-finite values.
Results may differ from a plain program's by a relative error of at most 0.017.
Values may be sent and summed in bfloat16 or wider, within the bound.
No kernel may reach another device: no remote copies, remote signals or barrier semaphores. Data moves between devices by JAX's collectives and lax.ppermute only.
A program may use at most 128 MiB of HBM per device.

v0:
```python
import math
import jax
import jax.numpy as jnp
from jax import lax
from jax.sharding import PartitionSpec as P

HEADS = 12
norm_epsilon = 1e-05
masked_score = -1e30


def alibi_slopes(head_count):
    nearest = 2 ** int(math.floor(math.log2(head_count)))
    base_list = [2.0 ** (-8.0 * (index + 1) / nearest) for index in range(nearest)]
    extra_list = [
        2.0 ** (-8.0 * (2 * index + 1) / (2 * nearest)) for index in range(head_count - nearest)
    ]
    return jnp.array(base_list + extra_list, dtype=jnp.float32)


def normalize(value, gain, shift):
    center = value - jnp.mean(value, axis=-1, keepdims=True)
    spread = jnp.mean(center * center, axis=-1, keepdims=True)
    return center * lax.rsqrt(spread + norm_epsilon) * gain + shift


def gated_unit(gate, up_half):
    return jax.nn.gelu(gate, approximate=False) * up_half


def score_block(query_blk, keys, seg_q, seg_k, pos_q, pos_k, slopes, scale):
    raw = jnp.einsum("qhd,khd->hqk", query_blk, keys, preferred_element_type=jnp.float32) * scale
    distance = jnp.abs(pos_q[:, None] - pos_k[None, :]).astype(jnp.float32)
    raw = raw - slopes[:, None, None] * distance[None]
    return jnp.where((seg_q[:, None] == seg_k[None, :])[None], raw, masked_score)


def local(
    tokens,
    segment_ids,
    masked_rows,
    replacement,
    cotangent,
    w_qkv,
    w_out_attn,
    w_in_ff,
    w_out_ff,
    gain_one,
    shift_one,
    gain_two,
    shift_two,
):
    rows_dev, width = tokens.shape
    ranks = lax.axis_size("sp")
    rank = lax.axis_index("sp")
    heads_local = HEADS // ranks
    head_dim = width // HEADS
    local_width = heads_local * head_dim
    hidden_width = w_out_ff.shape[0]
    scale = head_dim ** (-0.5)
    group_seg = segment_ids[0]
    group_tok = group_seg.shape[0]
    block = min(512, group_tok)
    count = group_tok // block
    positions = jnp.arange(group_tok, dtype=jnp.int32)
    slopes = lax.dynamic_slice_in_dim(alibi_slopes(HEADS), rank * heads_local, heads_local, 0)
    select = (jnp.arange(rows_dev, dtype=jnp.int32)[:, None] == masked_rows[None, :]).astype(
        jnp.float32
    )
    placed = jnp.dot(select, replacement.astype(jnp.float32), precision=lax.Precision.HIGHEST)
    hit = jnp.sum(select, axis=1, keepdims=True) > 0.5
    start_low = jnp.where(hit, placed, tokens.astype(jnp.float32)).astype(jnp.bfloat16)
    start = start_low.astype(jnp.float32)
    qkv = jnp.dot(start_low, w_qkv, preferred_element_type=jnp.float32).astype(jnp.bfloat16)
    qkv_heads = lax.all_to_all(
        qkv.reshape(rows_dev, 3, ranks, local_width), "sp", split_axis=2, concat_axis=0, tiled=True
    )
    qkv_heads = qkv_heads.reshape(group_tok, 3, heads_local, head_dim)
    query = qkv_heads[:, 0]
    keys = qkv_heads[:, 1]
    values = qkv_heads[:, 2]

    def forward_block(index):
        first = index * block
        query_blk = lax.dynamic_slice_in_dim(query, first, block, 0)
        seg_q = lax.dynamic_slice_in_dim(group_seg, first, block, 0)
        pos_q = lax.dynamic_slice_in_dim(positions, first, block, 0)
        scores = score_block(query_blk, keys, seg_q, group_seg, pos_q, positions, slopes, scale)
        peak = jnp.max(scores, axis=-1, keepdims=True)
        weights = jnp.exp(scores - peak)
        total = jnp.sum(weights, axis=-1, keepdims=True)
        probs = (weights / total).astype(jnp.bfloat16)
        out = jnp.einsum("hqk,khd->qhd", probs, values, preferred_element_type=jnp.float32)
        return (out.astype(jnp.bfloat16), (peak + jnp.log(total))[..., 0])

    attn_heads, logsum = lax.map(forward_block, jnp.arange(count, dtype=jnp.int32))
    attn_heads = attn_heads.reshape(group_tok, 1, local_width)
    attn_low = lax.all_to_all(attn_heads, "sp", split_axis=0, concat_axis=1, tiled=True).reshape(
        rows_dev, width
    )
    proj = jnp.dot(attn_low, w_out_attn, preferred_element_type=jnp.float32)
    first_norm, pull_one = jax.vjp(normalize, start + proj, gain_one, shift_one)
    first_low = first_norm.astype(jnp.bfloat16)
    mixed = jnp.dot(first_low, w_in_ff, preferred_element_type=jnp.float32)
    hidden, pull_gate = jax.vjp(gated_unit, mixed[:, :hidden_width], mixed[:, hidden_width:])
    hidden_low = hidden.astype(jnp.bfloat16)
    branch = jnp.dot(hidden_low, w_out_ff, preferred_element_type=jnp.float32)
    result, pull_two = jax.vjp(normalize, first_norm + branch, gain_two, shift_two)
    layer_out = result.astype(jnp.bfloat16)
    grad_result = jnp.dot(select, cotangent, precision=lax.Precision.HIGHEST)
    d_second, d_gain_two, d_shift_two = pull_two(grad_result)
    d_branch = d_second.astype(jnp.bfloat16)
    g_out_ff = jnp.einsum("tf,td->fd", hidden_low, d_branch, preferred_element_type=jnp.float32)
    d_hidden = jnp.einsum("td,fd->tf", d_branch, w_out_ff, preferred_element_type=jnp.float32)
    d_gate, d_up = pull_gate(d_hidden)
    d_mixed = jnp.concatenate([d_gate, d_up], axis=1).astype(jnp.bfloat16)
    g_in_ff = jnp.einsum("td,tf->df", first_low, d_mixed, preferred_element_type=jnp.float32)
    d_first = d_second + jnp.einsum(
        "tf,df->td", d_mixed, w_in_ff, preferred_element_type=jnp.float32
    )
    d_sum_one, d_gain_one, d_shift_one = pull_one(d_first)
    d_proj = d_sum_one.astype(jnp.bfloat16)
    g_out_attn = jnp.einsum("tc,td->cd", attn_low, d_proj, preferred_element_type=jnp.float32)
    d_attn = jnp.einsum("td,cd->tc", d_proj, w_out_attn, preferred_element_type=jnp.float32).astype(
        jnp.bfloat16
    )
    d_attn_heads = lax.all_to_all(
        d_attn.reshape(rows_dev, ranks, local_width), "sp", split_axis=1, concat_axis=0, tiled=True
    )
    d_attn_heads = d_attn_heads.reshape(group_tok, heads_local, head_dim)

    def backward_block(carry, index):
        d_keys, d_values = carry
        first = index * block
        query_blk = lax.dynamic_slice_in_dim(query, first, block, 0)
        dout_blk = lax.dynamic_slice_in_dim(d_attn_heads, first, block, 0)
        seg_q = lax.dynamic_slice_in_dim(group_seg, first, block, 0)
        pos_q = lax.dynamic_slice_in_dim(positions, first, block, 0)
        scores = score_block(query_blk, keys, seg_q, group_seg, pos_q, positions, slopes, scale)
        probs = jnp.exp(scores - logsum[index][:, :, None])
        d_probs = jnp.einsum("qhd,khd->hqk", dout_blk, values, preferred_element_type=jnp.float32)
        delta = jnp.sum(probs * d_probs, axis=-1, keepdims=True)
        d_scores = (probs * (d_probs - delta)).astype(jnp.bfloat16)
        d_query = (
            jnp.einsum("hqk,khd->qhd", d_scores, keys, preferred_element_type=jnp.float32) * scale
        )
        d_keys = (
            d_keys
            + jnp.einsum("hqk,qhd->khd", d_scores, query_blk, preferred_element_type=jnp.float32)
            * scale
        )
        d_values = d_values + jnp.einsum(
            "hqk,qhd->khd", probs.astype(jnp.bfloat16), dout_blk, preferred_element_type=jnp.float32
        )
        return ((d_keys, d_values), d_query)

    empty = jnp.zeros((group_tok, heads_local, head_dim), jnp.float32)
    (d_keys, d_values), d_query = lax.scan(
        backward_block, (empty, empty), jnp.arange(count, dtype=jnp.int32)
    )
    d_query = d_query.reshape(group_tok, heads_local, head_dim)
    d_qkv_heads = jnp.stack([d_query, d_keys, d_values], axis=1).astype(jnp.bfloat16)
    d_qkv = lax.all_to_all(
        d_qkv_heads.reshape(group_tok, 3, 1, local_width),
        "sp",
        split_axis=0,
        concat_axis=2,
        tiled=True,
    )
    d_qkv = d_qkv.reshape(rows_dev, 3 * width)
    g_qkv = jnp.einsum("tc,tq->cq", start_low, d_qkv, preferred_element_type=jnp.float32)
    d_start = d_sum_one + jnp.einsum("tq,cq->tc", d_qkv, w_qkv, preferred_element_type=jnp.float32)
    grad_tokens = jnp.where(hit, 0.0, d_start)
    grad_replacement = jnp.einsum("tm,tc->mc", select, d_start, precision=lax.Precision.HIGHEST)
    row_shares = (
        lax.psum_scatter(g_qkv, "dp", scatter_dimension=0, tiled=True),
        lax.psum_scatter(g_out_attn, "dp", scatter_dimension=0, tiled=True),
        lax.psum_scatter(g_in_ff, "dp", scatter_dimension=0, tiled=True),
        lax.psum_scatter(g_out_ff, "dp", scatter_dimension=0, tiled=True),
    )
    share_parts = (
        lax.psum_scatter(
            row_shares[0].astype(jnp.bfloat16), "sp", scatter_dimension=1, tiled=True
        ).astype(jnp.float32),
        lax.psum_scatter(
            row_shares[1].astype(jnp.bfloat16), "sp", scatter_dimension=1, tiled=True
        ).astype(jnp.float32),
        lax.psum_scatter(
            row_shares[2].astype(jnp.bfloat16), "sp", scatter_dimension=1, tiled=True
        ).astype(jnp.float32),
        lax.psum_scatter(
            row_shares[3].astype(jnp.bfloat16), "sp", scatter_dimension=1, tiled=True
        ).astype(jnp.float32),
    )
    summed = (
        lax.all_gather(share_parts[0].astype(jnp.bfloat16), "sp", axis=1, tiled=True).astype(
            jnp.float32
        ),
        lax.all_gather(share_parts[1].astype(jnp.bfloat16), "sp", axis=1, tiled=True).astype(
            jnp.float32
        ),
        lax.all_gather(share_parts[2].astype(jnp.bfloat16), "sp", axis=1, tiled=True).astype(
            jnp.float32
        ),
        lax.all_gather(share_parts[3].astype(jnp.bfloat16), "sp", axis=1, tiled=True).astype(
            jnp.float32
        ),
    )
    norm_sums = lax.psum((d_gain_one, d_shift_one, d_gain_two, d_shift_two), ("dp", "sp"))
    return (
        layer_out,
        grad_tokens,
        grad_replacement,
        summed[0],
        summed[1],
        summed[2],
        summed[3],
        norm_sums[0],
        norm_sums[1],
        norm_sums[2],
        norm_sums[3],
    )


def solution(mesh):
    return jax.shard_map(
        local,
        mesh=mesh,
        in_specs=(
            P(("dp", "sp"), None),
            P("dp", None),
            P(("dp", "sp")),
            P(("dp", "sp"), None),
            P(("dp", "sp"), None),
            P(),
            P(),
            P(),
            P(),
            P(),
            P(),
            P(),
            P(),
        ),
        out_specs=(
            P(("dp", "sp"), None),
            P(("dp", "sp"), None),
            P(("dp", "sp"), None),
            P("dp", None),
            P("dp", None),
            P("dp", None),
            P("dp", None),
            P(),
            P(),
            P(),
            P(),
        ),
        check_vma=False,
    )
```

profile of v0, /device:TPU:0, one launch (start us, length us, event | category | flops | bytes accessed | tf_op | source)
XLA Modules:
  0.0 950.8 jit_solution(5852370499418419649)
XLA Ops:
  13.0 2.4 copy.95
  15.4 2.4 copy.96
  17.7 4.3 all-to-all-start
  22.2 16.4 %all-to-all-done = bf16[256,3,4,192]{0,3,1,2:T(8,128)(2,1)} async-done(((bf16[256,3,4,192]{0,3,1,2:T(8,128)(2,1)}), bf16[256,3,4,192]{0,3,1,2:T(8,128)(2,1)}, u32[]{:S(2)}, u32[]{:S(2)}) %all-to-all-start) | async-done | bytes 1179680 | tf_op jit(solution)/shard_map/all_to_all | solution.py:75
  38.6 3.2 copy.97
  41.8 3.4 reshape.309
  45.2 2.3 slice_bitcast_fusion
  47.5 22.4 %while.29 = (s32[]{:T(128)}, bf16[2,512,3,64]{1,3,2,0:T(8,128)(2,1)}, f32[2,3,512]{2,1,0:T(4,128)}, s32[2]{0:T(128)S(1)}, s32[1024]{0:T(1024)S(1)}, /*index=5*/s...) while((s32[]{:T(128)}, ...), condition=%wide.region_4.5_spmd.clone, body=%wide.region_1.4_spmd.clone.sunk | while | flops 433158656 | bytes 32185620 | solution.py:96
  49.7 3.0 fusion.111
  52.7 2.2 fusion.112
  55.5 3.2 fusion.113
  60.9 3.0 fusion.111
  63.9 2.2 fusion.112
  66.7 3.2 fusion.113
  69.9 2.1 copy.98
  74.5 2.6 reduce
  79.1 2.4 reshape.324
  81.5 11.8 %all_to_all.60 = bf16[4,2,24576]{2,1,0:T(2,128)(2,1)} all-to-all(bf16[4,2,24576]{2,1,0:T(2,128)(2,1)} %reshape.324), channel_id=1, replica_groups=mesh['dp'=8,'sp'=4] {'sp'}, dimensions={0} | all-to-all | bytes 786432 | tf_op jit(solution)/shard_map/all_to_all | solution.py:98
  93.3 3.6 reshape.325
  96.9 3.5 copy.100
  106.4 5.4 fusion.57
  111.7 6.9 multiply_convert_fusion.2
  123.0 4.0 add_convert_fusion
  128.7 8.0 fusion.39
  137.4 8.6 multiply_reduce_fusion.2
  150.5 4.1 all-to-all-start.2
  154.6 3.2 fusion.55
  157.9 4.2 all-to-all-done.2
  166.7 67.6 %while.30 = (s32[]{:T(128)}, f32[1024,3,64]{0,2,1:T(8,128)}, f32[1024,3,64]{0,2,1:T(8,128)}, bf16[2,512,3,64]{1,3,2,0:T(8,128)(2,1)}, s32[2]{0:T(128)}, /*index=...) while((s32[]{:T(128)}, f32[1024,3,64]{0,2,1:T(8,128)}, ...), condition=%wide.region_15.16_spmd.clone.clone, body=%wide.region_13.15_spmd.clone.clone.sunk | while | flops 1027111424 | bytes 128764864 | solution.py:158
  168.7 4.8 fusion.123
  179.2 6.9 multiply_reduce_fusion.8
  186.0 2.6 copy-done.1
  188.6 2.3 multiply_convert_fusion.4
  191.0 3.7 fusion.124
  194.7 3.8 fusion.126
  201.9 4.8 fusion.123
  212.3 6.7 multiply_reduce_fusion.8
  219.0 2.6 copy-done.1
  221.6 2.3 multiply_convert_fusion.4
  223.9 3.9 fusion.124
  227.8 3.7 fusion.126
  231.5 2.7 fusion.125
  234.2 2.1 copy.104
  243.0 4.1 copy.105
  247.0 30.1 %all_to_all.61 = bf16[1024,3,1,192]{3,1,2,0:T(4,128)(2,1)} all-to-all(bf16[1024,3,1,192]{3,1,2,0:T(4,128)(2,1)} %copy.105), channel_id=1, replica_groups=mesh['dp'=8,'sp'=4] {'sp'}, dimensions={0} | all-to-all | bytes 2359296 | tf_op jit(solution)/shard_map/all_to_all | solution.py:163
  277.2 4.3 copy.113
  283.9 5.0 fusion.64
  289.6 6.9 fusion.53
  296.5 154.8 %reduce-scatter.19.cloned.1.call-done = f32[96,6144]{1,0:T(8,128)} async-done(((f32[768,6144]{1,0:T(8,128)}), f32[96,6144]{1,0:T(8,128)}) %reduce-scatter.19.cloned.1.call-update) | async-done | bytes 2359312 | tf_op jit(solution)/shard_map/reduce_scatter | solution.py:178
  451.3 2.8 convert_element_type.119
  454.2 69.2 %reduce-scatter.17.cloned.1.call-done = f32[96,768]{1,0:T(8,128)} async-done(((f32[768,768]{1,0:T(8,128)}), f32[96,768]{1,0:T(8,128)}) %reduce-scatter.17.cloned.1.call-update) | async-done | bytes 294928 | tf_op jit(solution)/shard_map/reduce_scatter | solution.py:177
  526.8 128.3 %reduce-scatter.15.cloned.1.call-done = f32[96,2304]{1,0:T(8,128)} async-done(((f32[768,2304]{1,0:T(8,128)}), f32[96,2304]{1,0:T(8,128)}) %reduce-scatter.15.cloned.1.call-update) | async-done | bytes 884752 | tf_op jit(solution)/shard_map/reduce_scatter | solution.py:176
  659.6 161.9 %reduce-scatter.23.cloned.1.call-done = f32[384,768]{1,0:T(8,128)} async-done(((f32[3072,768]{1,0:T(8,128)}), f32[384,768]{1,0:T(8,128)}) %reduce-scatter.23.cloned.1.call-update) | async-done | bytes 1179664 | tf_op jit(solution)/shard_map/reduce_scatter | solution.py:179
  825.8 23.2 %reduce-scatter.21.cloned.1.call-done = bf16[96,1536]{1,0:T(8,128)(2,1)} async-done(((bf16[96,6144]{1,0:T(8,128)(2,1)}), bf16[96,1536]{1,0:T(8,128)(2,1)}) %reduce-scatter.21.cloned.1.call-update) | async-done | bytes 294928 | tf_op jit(solution)/shard_map/reduce_scatter | solution.py:188
  849.0 39.8 %all-reduce = (f32[768]{0:T(1024)}, f32[768]{0:T(1024)}, f32[768]{0:T(1024)}, f32[768]{0:T(1024)}) all-reduce(f32[768]{0:T(1024)} %get-tuple-element.303, f32[768]{0:T(1024)} %get-tuple-element.306, f32[768]{0:T(1024)S(1)} %copy-done.25, f32[768]{0:T(1024)S(1)} %copy-done.26), channel_id=1, replica_groups=mesh['dp'=8,'sp'=4] {'dp','sp'}, use_global_device_ids=true, to_apply=%region_25.26 | all-reduce | flops 3072 | bytes 24576 | tf_op jit(solution)/shard_map/psum | solution.py:209
  888.8 3.5 broadcast_select_fusion
  893.5 8.6 all_gather.13
  905.5 7.3 all-gather
  914.0 2.7 reshape.317
  916.7 5.2 reduce-scatter.29.cloned.1.call-done
  921.9 8.1 all_gather.15
  930.0 2.3 copy.112
  932.3 8.7 all-gather.3.cloned.1.call-done
  941.0 2.9 convert_element_type.120
  (193 shorter events, 75.4 us)
Async XLA Ops:
  7.2 3.7 copy-start
  8.1 0.6 copy-start.27
  10.1 0.7 copy-start.11
  13.0 9.1 copy-start.36
  17.7 20.8 %all-to-all-start = ((bf16[256,3,4,192]{0,3,1,2:T(8,128)(2,1)}), bf16[256,3,4,192]{0,3,1,2:T(8,128)(2,1)}, u32[]{:S(2)}, u32[]{:S(2)}) async-start(bf16[256,3,4,192]{0,3,1,2:T(8,128)(2,1)} %copy.96), calls=%async_computation | async-start | bytes 2359296 | tf_op jit(solution)/shard_map/all_to_all | solution.py:75
  22.0 429.3 %reduce-scatter.19.cloned.1.call-start = ((), (), s32[]{:S(2)}) async-start(), calls=%async_computation.14 | async-start | bytes 21233664 | tf_op jit(solution)/shard_map/reduce_scatter | solution.py:178
  38.6 8.9 copy-start.16
  52.7 2.8 copy-start.6
  63.9 2.8 copy-start.6
  69.9 23.4 %copy-start.22 = (f32[3]{0:T(128)}, f32[3]{0:T(128)S(1)}, u32[]{:S(2)}) copy-start(f32[3]{0:T(128)S(1)} %get-tuple-element.690) | copy-start | bytes 40
  96.9 9.5 copy-start.17
  96.9 9.5 copy-start.18
  103.4 2.4 copy-start.12
  103.4 15.3 %slice-start.2 = ((s8[4718592]{0:T(1024)(128)(4,1)}), s8[4194304]{0:T(1024)(128)(4,1)S(1)}, s32[]{:S(2)}) async-start(s8[4718592]{0:T(1024)(128)(4,1)} %bitcast.161), calls=%async_computation.23 | async-start | bytes 8388608
  105.5 21.5 %copy-start.3 = (f32[256,768]{1,0:T(8,128)}, f32[256,768]{1,0:T(8,128)S(1)}, u32[]{:S(2)}) copy-start(f32[256,768]{1,0:T(8,128)S(1)} %get-tuple-element.378) | copy-start | bytes 2359300
  105.8 0.5 copy-start.29
  106.3 20.8 %copy-start.20 = (f32[256]{0:T(256)}, f32[256]{0:T(256)S(1)}, u32[]{:S(2)}) copy-start(f32[256]{0:T(256)S(1)} %fusion.49) | copy-start | bytes 3076
  106.3 12.3 %slice-start.3 = ((s8[4718592]{0:T(1024)(128)(4,1)}), s8[524288]{0:T(1024)(128)(4,1)S(1)}, s32[]{:S(2)}) async-start(s8[4718592]{0:T(1024)(128)(4,1)} %bitcast.161), calls=%async_computation.24 | async-start | bytes 1048576
  118.7 1.6 copy-start.9
  118.7 1.8 copy-start.19
  118.7 1.8 copy-start.24
  118.7 1.8 copy-start.31
  118.7 3.2 copy-start.33
  123.0 4.0 copy-start.13
  123.0 4.0 copy-start.34
  127.1 1.2 copy-start.14
  127.1 1.7 copy-start.15
  136.7 0.7 copy-start.21
  137.4 8.6 copy-start.30
  137.4 8.6 copy-start.4
  137.4 9.9 %copy-start.10 = (bf16[768,768]{1,0:T(8,128)(2,1)S(1)}, bf16[768,768]{1,0:T(8,128)(2,1)}, u32[]{:S(2)}) copy-start(bf16[768,768]{1,0:T(8,128)(2,1)} %param.24) | copy-start | bytes 3538948
  146.4 0.9 copy-start.7
  150.5 11.6 %all-to-all-start.2 = ((bf16[256,4,192]{0,2,1:T(8,128)(2,1)}), bf16[256,4,192]{0,2,1:T(8,128)(2,1)}, u32[]{:S(2)}, u32[]{:S(2)}) async-start(bf16[256,4,192]{0,2,1:T(8,128)(2,1)} %bitcast.143), calls=%async_computation.2 | async-start | bytes 786432 | tf_op jit(solution)/shard_map/all_to_all | solution.py:127
  154.6 12.1 %copy-start.23 = (f32[3]{0:T(128)S(1)}, f32[3]{0:T(128)}, u32[]{:S(2)}) copy-start(f32[3]{0:T(128)} %copy-done.22) | copy-start | bytes 40
  154.6 368.8 %reduce-scatter.17.cloned.1.call-start = ((), (), s32[]{:S(2)}) async-start(), calls=%async_computation.13 | async-start | bytes 2654208 | tf_op jit(solution)/shard_map/reduce_scatter | solution.py:177
  157.9 497.3 %reduce-scatter.15.cloned.1.call-start = ((), (), s32[]{:S(2)}) async-start(), calls=%async_computation.12 | async-start | bytes 7962624 | tf_op jit(solution)/shard_map/reduce_scatter | solution.py:176
  179.1 9.5 slice-start
  179.1 9.5 slice-start.1
  186.0 2.6 copy-start.1
  191.0 7.5 copy-start.2
  194.7 3.8 copy-start.5
  212.3 9.3 slice-start
  212.3 9.3 slice-start.1
  219.0 2.6 copy-start.1
  223.9 7.6 copy-start.2
  227.8 3.8 copy-start.5
  282.9 1.0 copy-start.8
  288.9 0.7 copy-start.35
  288.9 532.5 %reduce-scatter.23.cloned.1.call-start = ((), (), s32[]{:S(2)}) async-start(), calls=%async_computation.17 | async-start | bytes 10616832 | tf_op jit(solution)/shard_map/reduce_scatter | solution.py:179
  296.4 552.5 %reduce-scatter.21.cloned.1.call-start = ((), (), s32[]{:S(2)}) async-start(), calls=%async_computation.15 | async-start | bytes 1474560 | tf_op jit(solution)/shard_map/reduce_scatter | solution.py:188
  454.1 439.3 %reduce-scatter.27.cloned.1.call-start = ((), (), s32[]{:S(2)}) async-start(), calls=%async_computation.19 | async-start | bytes 245760
  526.8 322.2 %copy-start.25 = (f32[768]{0:T(1024)S(1)}, f32[768]{0:T(1024)}, u32[]{:S(2)}) copy-start(f32[768]{0:T(1024)} %get-tuple-element.301) | copy-start | bytes 9220
  526.8 322.2 %copy-start.26 = (f32[768]{0:T(1024)S(1)}, f32[768]{0:T(1024)}, u32[]{:S(2)}) copy-start(f32[768]{0:T(1024)} %get-tuple-element.305) | copy-start | bytes 9220
  526.8 362.0 %copy-start.28 = (pred[256]{0:T(512)(128)(4,1)S(1)}, pred[256]{0:T(512)(128)(4,1)}, u32[]{:S(2)}) copy-start(pred[256]{0:T(512)(128)(4,1)} %copy-done.27) | copy-start | bytes 772
  526.8 377.0 %reduce-scatter.25.cloned.1.call-start = ((), (), s32[]{:S(2)}) async-start(), calls=%async_computation.18 | async-start | bytes 737280
  659.3 262.6 %reduce-scatter.29.cloned.1.call-start = ((), (), s32[]{:S(2)}) async-start(), calls=%async_computation.20 | async-start | bytes 737280
  825.7 115.2 %all-gather.3.cloned.1.call-start = ((), (), s32[]{:S(2)}) async-start(), calls=%async_computation.16 | async-start | bytes 1474560 | tf_op jit(solution)/shard_map/all_gather | solution.py:202
  888.8 3.5 copy-start.32
Sparse Core Ops, SparseCore 0:
  136.8 314.3 reduce-scatter.18
  455.4 67.9 reduce-scatter.16
  527.1 128.0 reduce-scatter.14
  659.1 162.3 reduce-scatter.22
  824.0 24.8 reduce-scatter.20
  851.8 19.7 reduce-scatter.26
  874.6 22.0 reduce-scatter.24
  899.8 22.0 reduce-scatter.28
  923.4 17.4 all-gather.2
where the time goes:
time: 961 us; the launch traced here: 951 us
  waiting for transfers between devices  572 us (60%)
  matrix products  111 us (12%)
  blocking collectives  106 us (11%)
  local copies, waits for them, and re-layouts  86.4 us (9%)
  other arithmetic  45.7 us (5%)
  between operations  14.8 us (2%)
    reduce_scatter x1, waiting for transfers between devices, local(): lax.psum_scatter(g_out_ff, 'dp', scatter_dimension=0, tiled=True)  162 us
    reduce_scatter x1, waiting for transfers between devices, local(): lax.psum_scatter(g_in_ff, 'dp', scatter_dimension=0, tiled=True)  155 us
    reduce_scatter x1, waiting for transfers between devices, local(): lax.psum_scatter(g_qkv, 'dp', scatter_dimension=0, tiled=True)  128 us
    reduce_scatter x1, waiting for transfers between devices, local(): lax.psum_scatter(g_out_attn, 'dp', scatter_dimension=0, tiled=True)  69.2 us
    psum x1, blocking collectives, local(): lax.psum((d_gain_one, d_shift_one, d_gain_two, d_shift_two), ('dp', 'sp'))  39.8 us
    all_to_all x1, blocking collectives, local(): lax.all_to_all(d_qkv_heads.reshape(group_tok, 3, 1, local_width), 'sp', s...  30.1 us
    unnamed x79, local copies, waits for them, and re-layouts  26.3 us
    reduce_scatter x1, waiting for transfers between devices, local(): lax.psum_scatter(row_shares[2].astype(jnp.bfloat16), 'sp', scatter_dimens...  23.2 us
  transfers between devices with their start and end apart: 11, of which 9 were waited for; matrix products, arithmetic and copies ran while one was open for 14% of the time, Pallas kernels for 0%

commit v1 on v0

--- a/solution.py
+++ b/solution.py
@@ -160,12 +160,18 @@
     )
     d_query = d_query.reshape(group_tok, heads_local, head_dim)
     d_qkv_heads = jnp.stack([d_query, d_keys, d_values], axis=1).astype(jnp.bfloat16)
-    d_qkv = lax.all_to_all(
-        d_qkv_heads.reshape(group_tok, 3, 1, local_width),
-        "sp",
-        split_axis=0,
-        concat_axis=2,
-        tiled=True,
+    d_qkv = jnp.concatenate(
+        lax.all_to_all(
+            jnp.stack(
+                jnp.split(
+                    d_qkv_heads.reshape(group_tok, 3, 1, local_width), lax.axis_size("sp"), axis=0
+                )
+            ),
+            "sp",
+            0,
+            0,
+        ),
+        axis=2,
     )
     d_qkv = d_qkv.reshape(rows_dev, 3 * width)
     g_qkv = jnp.einsum("tc,tq->cq", start_low, d_qkv, preferred_element_type=jnp.float32)

time: 961 us -> 961 us (level)
  waiting for transfers between devices: 572 us -> 596 us
  blocking collectives: 106 us -> 93.8 us
    reduce_scatter x1, waiting for transfers between devices: 155 us -> 179 us  [local(): lax.psum_scatter(g_in_ff, 'dp', scatter_dimension=0, tiled=True)]
    all_to_all x1, blocking collectives: 30.1 us -> 18.3 us  [local(): lax.all_to_all(jnp.stack(jnp.split(d_qkv_heads.reshape(group_tok, 3, 1, l...]
    unnamed x79 -> x81, local copies, waits for them, and re-layouts: 26.3 us -> 26.4 us
  transfers between devices with their start and end apart: 11 -> 11, of which waited for: 9 -> 9; matrix products, arithmetic and copies ran while one was open for 14% -> 13% of each run, Pallas kernels for 0% -> 0%
where the time goes in v1:
time: 961 us; the launch traced here: 951 us
  waiting for transfers between devices  596 us (62%)
  matrix products  110 us (11%)
  blocking collectives  93.8 us (10%)
  local copies, waits for them, and re-layouts  76.9 us (8%)
  other arithmetic  44.1 us (5%)
  between operations  14.8 us (2%)
    reduce_scatter x1, waiting for transfers between devices, local(): lax.psum_scatter(g_in_ff, 'dp', scatter_dimension=0, tiled=True)  179 us
    reduce_scatter x1, waiting for transfers between devices, local(): lax.psum_scatter(g_out_ff, 'dp', scatter_dimension=0, tiled=True)  162 us
    reduce_scatter x1, waiting for transfers between devices, local(): lax.psum_scatter(g_qkv, 'dp', scatter_dimension=0, tiled=True)  128 us
    reduce_scatter x1, waiting for transfers between devices, local(): lax.psum_scatter(g_out_attn, 'dp', scatter_dimension=0, tiled=True)  69.4 us
    psum x1, blocking collectives, local(): lax.psum((d_gain_one, d_shift_one, d_gain_two, d_shift_two), ('dp', 'sp'))  39.8 us
    unnamed x81, local copies, waits for them, and re-layouts  26.4 us
    reduce_scatter x1, waiting for transfers between devices, local(): lax.psum_scatter(row_shares[2].astype(jnp.bfloat16), 'sp', scatter_dimens...  22.8 us
    dot_general x4, matrix products, score_block(): jnp.einsum('qhd,khd->hqk', query_blk, keys, preferred_element_type=jnp.fl...  19.6 us
  transfers between devices with their start and end apart: 11, of which 9 were waited for; matrix products, arithmetic and copies ran while one was open for 13% of the time, Pallas kernels for 0%

profile of v1, /device:TPU:0, one launch (start us, length us, event | category | flops | bytes accessed | tf_op | source)
XLA Modules:
  0.0 951.2 jit_solution(16681458833604609142)
XLA Ops:
  10.8 2.1 convolution_convert_fusion
  13.0 2.4 copy.65
  15.3 2.4 copy.66
  17.7 4.3 all-to-all-start
  22.1 16.4 %all-to-all-done = bf16[256,3,4,192]{0,3,1,2:T(8,128)(2,1)} async-done(((bf16[256,3,4,192]{0,3,1,2:T(8,128)(2,1)}), bf16[256,3,4,192]{0,3,1,2:T(8,128)(2,1)}, u32[]{:S(2)}, u32[]{:S(2)}) %all-to-all-start) | async-done | bytes 1179680 | tf_op jit(solution)/shard_map/all_to_all | solution.py:75
  38.6 3.2 copy.67
  41.8 3.4 reshape.268
  45.2 2.3 slice_bitcast_fusion
  47.5 22.4 %while.29 = (s32[]{:T(128)}, bf16[2,512,3,64]{1,3,2,0:T(8,128)(2,1)}, f32[2,3,512]{2,1,0:T(4,128)}, s32[2]{0:T(128)S(1)}, s32[1024]{0:T(1024)S(1)}, /*index=5*/s...) while((s32[]{:T(128)}, ...), condition=%wide.region_4.5_spmd.clone, body=%wide.region_1.4_spmd.clone.sunk | while | flops 433158656 | bytes 32185620 | solution.py:96
  49.7 3.0 fusion.112
  52.7 2.2 fusion.113
  55.5 3.2 fusion.114
  60.9 3.0 fusion.112
  63.9 2.2 fusion.113
  66.7 3.2 fusion.114
  69.9 2.1 copy.68
  74.6 2.6 reduce
  79.1 2.4 reshape.283
  81.5 11.8 %all_to_all.50 = bf16[4,2,24576]{2,1,0:T(2,128)(2,1)} all-to-all(bf16[4,2,24576]{2,1,0:T(2,128)(2,1)} %reshape.283), channel_id=1, replica_groups=mesh['dp'=8,'sp'=4] {'sp'}, dimensions={0} | all-to-all | bytes 786432 | tf_op jit(solution)/shard_map/all_to_all | solution.py:98
  93.3 3.6 reshape.284
  96.9 3.5 copy.70
  106.4 5.4 fusion.57
  111.8 6.9 multiply_convert_fusion.2
  123.1 4.0 add_convert_fusion
  128.8 8.1 fusion.39
  137.6 8.6 multiply_reduce_fusion.2
  150.7 4.1 all-to-all-start.2
  154.9 3.2 fusion.55
  158.1 4.2 all-to-all-done.2
  166.9 67.4 %while.30 = (s32[]{:T(128)}, f32[1024,3,64]{0,2,1:T(8,128)}, f32[1024,3,64]{0,2,1:T(8,128)}, bf16[2,512,3,64]{1,3,2,0:T(8,128)(2,1)}, s32[2]{0:T(128)}, /*index=...) while((s32[]{:T(128)}, f32[1024,3,64]{0,2,1:T(8,128)}, ...), condition=%wide.region_15.16_spmd.clone.clone, body=%wide.region_13.15_spmd.clone.clone.sunk | while | flops 1027111424 | bytes 128764864 | solution.py:158
  168.9 4.8 fusion.124
  179.2 6.9 multiply_reduce_fusion.8
  186.1 2.6 copy-done.1
  188.7 2.3 multiply_convert_fusion.4
  191.1 3.7 fusion.125
  194.8 3.8 fusion.127
  201.9 4.8 fusion.124
  212.3 6.7 multiply_reduce_fusion.8
  219.0 2.6 copy-done.1
  221.6 2.3 multiply_convert_fusion.4
  224.0 3.9 fusion.125
  227.8 3.7 fusion.127
  231.6 2.7 fusion.126
  234.3 2.1 copy.74
  241.4 18.3 %all_to_all.51 = bf16[4,256,3,1,192]{1,4,2,3,0:T(8,128)(2,1)S(1)} all-to-all(bf16[4,256,3,1,192]{1,4,2,3,0:T(8,128)(2,1)S(1)} %pad_maximum_fusion.6), channel_id=1, replica_groups=mesh['dp'=8,'sp'=4] {'sp'}, dimensions={0} | all-to-all | bytes 2359296 | tf_op jit(solution)/shard_map/all_to_all | solution.py:164
  260.8 4.0 fusion.65
  265.5 6.8 fusion.53
  272.4 179.0 %reduce-scatter.19.cloned.1.call-done = f32[96,6144]{1,0:T(8,128)} async-done(((f32[768,6144]{1,0:T(8,128)}), f32[96,6144]{1,0:T(8,128)}) %reduce-scatter.19.cloned.1.call-update) | async-done | bytes 2359312 | tf_op jit(solution)/shard_map/reduce_scatter | solution.py:184
  451.4 2.8 convert_element_type.112
  454.3 69.4 %reduce-scatter.17.cloned.1.call-done = f32[96,768]{1,0:T(8,128)} async-done(((f32[768,768]{1,0:T(8,128)}), f32[96,768]{1,0:T(8,128)}) %reduce-scatter.17.cloned.1.call-update) | async-done | bytes 294928 | tf_op jit(solution)/shard_map/reduce_scatter | solution.py:183
  527.2 128.3 %reduce-scatter.15.cloned.1.call-done = f32[96,2304]{1,0:T(8,128)} async-done(((f32[768,2304]{1,0:T(8,128)}), f32[96,2304]{1,0:T(8,128)}) %reduce-scatter.15.cloned.1.call-update) | async-done | bytes 884752 | tf_op jit(solution)/shard_map/reduce_scatter | solution.py:182
  659.5 162.3 %reduce-scatter.23.cloned.1.call-done = f32[384,768]{1,0:T(8,128)} async-done(((f32[3072,768]{1,0:T(8,128)}), f32[384,768]{1,0:T(8,128)}) %reduce-scatter.23.cloned.1.call-update) | async-done | bytes 1179664 | tf_op jit(solution)/shard_map/reduce_scatter | solution.py:185
  821.9 2.1 convert_element_type.114
  826.5 22.8 %reduce-scatter.21.cloned.1.call-done = bf16[96,1536]{1,0:T(8,128)(2,1)} async-done(((bf16[96,6144]{1,0:T(8,128)(2,1)}), bf16[96,1536]{1,0:T(8,128)(2,1)}) %reduce-scatter.21.cloned.1.call-update) | async-done | bytes 294928 | tf_op jit(solution)/shard_map/reduce_scatter | solution.py:194
  849.3 39.8 %all-reduce = (f32[768]{0:T(1024)}, f32[768]{0:T(1024)}, f32[768]{0:T(1024)}, f32[768]{0:T(1024)}) all-reduce(f32[768]{0:T(1024)} %get-tuple-element.281, f32[768]{0:T(1024)} %get-tuple-element.284, f32[768]{0:T(1024)S(1)} %copy-done.26, f32[768]{0:T(1024)S(1)} %copy-done.27), channel_id=1, replica_groups=mesh['dp'=8,'sp'=4] {'dp','sp'}, use_global_device_ids=true, to_apply=%region_25.26 | all-reduce | flops 3072 | bytes 24576 | tf_op jit(solution)/shard_map/psum | solution.py:215
  889.2 3.5 broadcast_select_fusion
  893.8 8.6 all_gather.13
  905.8 7.3 all-gather
  914.3 2.7 reshape.276
  917.1 5.2 reduce-scatter.29.cloned.1.call-done
  922.3 8.1 all_gather.15
  930.4 2.3 copy.80
  932.7 8.7 all-gather.3.cloned.1.call-done
  941.4 2.9 convert_element_type.113
  (194 shorter events, 68.2 us)
Async XLA Ops:
  7.2 3.7 copy-start
  8.1 0.5 copy-start.28
  10.1 0.7 copy-start.11
  13.0 9.1 copy-start.37
  17.7 20.9 %all-to-all-start = ((bf16[256,3,4,192]{0,3,1,2:T(8,128)(2,1)}), bf16[256,3,4,192]{0,3,1,2:T(8,128)(2,1)}, u32[]{:S(2)}, u32[]{:S(2)}) async-start(bf16[256,3,4,192]{0,3,1,2:T(8,128)(2,1)} %copy.66), calls=%async_computation | async-start | bytes 2359296 | tf_op jit(solution)/shard_map/all_to_all | solution.py:75
  22.0 429.4 %reduce-scatter.19.cloned.1.call-start = ((), (), s32[]{:S(2)}) async-start(), calls=%async_computation.14 | async-start | bytes 21233664 | tf_op jit(solution)/shard_map/reduce_scatter | solution.py:184
  38.6 8.9 copy-start.17
  52.7 2.8 copy-start.6
  63.9 2.8 copy-start.6
  69.9 23.4 %copy-start.23 = (f32[3]{0:T(128)}, f32[3]{0:T(128)S(1)}, u32[]{:S(2)}) copy-start(f32[3]{0:T(128)S(1)} %get-tuple-element.674) | copy-start | bytes 40
  96.9 9.5 %copy-start.18 = (f32[768]{0:T(1024)S(1)}, f32[768]{0:T(1024)}, u32[]{:S(2)}) copy-start(f32[768]{0:T(1024)} %param.27) | copy-start | bytes 9220
  96.9 9.5 %copy-start.19 = (f32[768]{0:T(1024)S(1)}, f32[768]{0:T(1024)}, u32[]{:S(2)}) copy-start(f32[768]{0:T(1024)} %param.28) | copy-start | bytes 9220
  103.4 2.4 copy-start.13
  103.4 15.3 %slice-start.2 = ((s8[4718592]{0:T(1024)(128)(4,1)}), s8[4194304]{0:T(1024)(128)(4,1)S(1)}, s32[]{:S(2)}) async-start(s8[4718592]{0:T(1024)(128)(4,1)} %bitcast.167), calls=%async_computation.23 | async-start | bytes 8388608
  105.6 21.6 %copy-start.3 = (f32[256,768]{1,0:T(8,128)}, f32[256,768]{1,0:T(8,128)S(1)}, u32[]{:S(2)}) copy-start(f32[256,768]{1,0:T(8,128)S(1)} %get-tuple-element.360) | copy-start | bytes 2359300
  105.8 0.6 copy-start.30
  106.4 20.8 %copy-start.21 = (f32[256]{0:T(256)}, f32[256]{0:T(256)S(1)}, u32[]{:S(2)}) copy-start(f32[256]{0:T(256)S(1)} %fusion.49) | copy-start | bytes 3076
  106.4 12.3 %slice-start.3 = ((s8[4718592]{0:T(1024)(128)(4,1)}), s8[524288]{0:T(1024)(128)(4,1)S(1)}, s32[]{:S(2)}) async-start(s8[4718592]{0:T(1024)(128)(4,1)} %bitcast.167), calls=%async_computation.24 | async-start | bytes 1048576
  118.7 1.6 copy-start.9
  118.8 1.8 copy-start.20
  118.8 1.8 copy-start.25
  118.8 1.8 copy-start.32
  118.8 3.2 copy-start.34
  123.1 4.0 copy-start.14
  123.1 4.0 copy-start.35
  127.1 1.2 copy-start.15
  127.1 1.7 copy-start.16
  136.9 0.7 copy-start.22
  137.6 8.6 copy-start.31
  137.6 8.7 copy-start.4
  137.6 9.9 %copy-start.10 = (bf16[768,768]{1,0:T(8,128)(2,1)S(1)}, bf16[768,768]{1,0:T(8,128)(2,1)}, u32[]{:S(2)}) copy-start(bf16[768,768]{1,0:T(8,128)(2,1)} %param.24) | copy-start | bytes 3538948
  146.6 0.9 copy-start.7
  150.7 11.6 %all-to-all-start.2 = ((bf16[256,4,192]{0,2,1:T(8,128)(2,1)}), bf16[256,4,192]{0,2,1:T(8,128)(2,1)}, u32[]{:S(2)}, u32[]{:S(2)}) async-start(bf16[256,4,192]{0,2,1:T(8,128)(2,1)} %bitcast.147), calls=%async_computation.2 | async-start | bytes 786432 | tf_op jit(solution)/shard_map/all_to_all | solution.py:127
  154.8 12.1 %copy-start.24 = (f32[3]{0:T(128)S(1)}, f32[3]{0:T(128)}, u32[]{:S(2)}) copy-start(f32[3]{0:T(128)} %copy-done.23) | copy-start | bytes 40
  154.8 368.9 %reduce-scatter.17.cloned.1.call-start = ((), (), s32[]{:S(2)}) async-start(), calls=%async_computation.13 | async-start | bytes 2654208 | tf_op jit(solution)/shard_map/reduce_scatter | solution.py:183
  158.1 497.3 %reduce-scatter.15.cloned.1.call-start = ((), (), s32[]{:S(2)}) async-start(), calls=%async_computation.12 | async-start | bytes 7962624 | tf_op jit(solution)/shard_map/reduce_scatter | solution.py:182
  179.2 9.5 slice-start
  179.2 9.5 slice-start.1
  186.1 2.6 copy-start.1
  191.1 7.5 copy-start.2
  194.8 3.8 copy-start.5
  212.3 9.3 slice-start
  212.3 9.3 slice-start.1
  219.0 2.6 copy-start.1
  224.0 7.6 copy-start.2
  227.8 3.7 copy-start.5
  241.2 19.6 %copy-start.12 = (bf16[256,768]{1,0:T(8,128)(2,1)S(1)}, bf16[256,768]{1,0:T(8,128)(2,1)}, u32[]{:S(2)}) copy-start(bf16[256,768]{1,0:T(8,128)(2,1)} %copy-done.11) | copy-start | bytes 1179652
  259.8 1.0 copy-start.8
  264.8 0.7 copy-start.36
  264.8 557.0 %reduce-scatter.23.cloned.1.call-start = ((), (), s32[]{:S(2)}) async-start(), calls=%async_computation.17 | async-start | bytes 10616832 | tf_op jit(solution)/shard_map/reduce_scatter | solution.py:185
  272.4 576.9 %reduce-scatter.21.cloned.1.call-start = ((), (), s32[]{:S(2)}) async-start(), calls=%async_computation.15 | async-start | bytes 1474560 | tf_op jit(solution)/shard_map/reduce_scatter | solution.py:194
  454.3 439.6 %reduce-scatter.27.cloned.1.call-start = ((), (), s32[]{:S(2)}) async-start(), calls=%async_computation.19 | async-start | bytes 245760
  527.1 322.2 %copy-start.26 = (f32[768]{0:T(1024)S(1)}, f32[768]{0:T(1024)}, u32[]{:S(2)}) copy-start(f32[768]{0:T(1024)} %get-tuple-element.279) | copy-start | bytes 9220
  527.1 322.2 %copy-start.27 = (f32[768]{0:T(1024)S(1)}, f32[768]{0:T(1024)}, u32[]{:S(2)}) copy-start(f32[768]{0:T(1024)} %get-tuple-element.283) | copy-start | bytes 9220
  527.1 362.1 %copy-start.29 = (pred[256]{0:T(512)(128)(4,1)S(1)}, pred[256]{0:T(512)(128)(4,1)}, u32[]{:S(2)}) copy-start(pred[256]{0:T(512)(128)(4,1)} %copy-done.28) | copy-start | bytes 772
  527.1 377.0 %reduce-scatter.25.cloned.1.call-start = ((), (), s32[]{:S(2)}) async-start(), calls=%async_computation.18 | async-start | bytes 737280
  659.5 262.8 %reduce-scatter.29.cloned.1.call-start = ((), (), s32[]{:S(2)}) async-start(), calls=%async_computation.20 | async-start | bytes 737280
  826.2 115.2 %all-gather.3.cloned.1.call-start = ((), (), s32[]{:S(2)}) async-start(), calls=%async_computation.16 | async-start | bytes 1474560 | tf_op jit(solution)/shard_map/all_gather | solution.py:208
  889.2 3.5 copy-start.33
Sparse Core Ops, SparseCore 0:
  137.0 314.3 reduce-scatter.18
  455.5 68.1 reduce-scatter.16
  527.4 128.0 reduce-scatter.14
  659.3 162.5 reduce-scatter.22
  824.5 24.7 reduce-scatter.20
  852.2 19.7 reduce-scatter.26
  875.0 22.0 reduce-scatter.24
  900.2 22.0 reduce-scatter.28
  923.9 17.4 all-gather.2
